TPU v7x, 256 devices: a whole 4x4x8 slice. The times are simulated.
256 devices in a mesh: req: 64 (over y, z, core), rep: 4 (over x).
Axes of the slice: x: 4, y: 4, z: 8, core: 2. Of those that a mesh axis runs over, the one named last changes fastest.
Arguments:
- hidden: bfloat16 [512, 64, 1152], P('rep', 'req'), may hold values from -6 to 6
- norm_gain: float32 [1152], replicated, may hold values from 0.1 to 1.9
- w_qkv: bfloat16 [1152, 1920], replicated, may hold values from -0.1875 to 0.1875
- w_out: bfloat16 [1152, 1152], replicated, may hold values from -0.1875 to 0.1875
- ffn_gain: float32 [1152], replicated, may hold values from 0.1 to 1.9
- w_gate: bfloat16 [1152, 1536], P(None, 'rep'), may hold values from -0.1875 to 0.1875
- w_up: bfloat16 [1152, 1536], P(None, 'rep'), may hold values from -0.1875 to 0.1875
- w_down: bfloat16 [1536, 1152], P('rep'), may hold values from -0.15625 to 0.15625
- cache: bfloat16 [4096, 2, 128, 384], P(('req', 'rep')), may hold values from -363 to 363, as said below
- page_table: int32 [512, 4, 5], P('req', 'rep'), may hold values from 0 to 15, as said below
- cache_len: int32 [512], P('req'), may hold values from 2049 to 2560, as said below
- parents: int32 [512, 64], P('req'), may hold values from 0 to 62, as said below
- accept_leaf: int32 [512], P('req'), may hold values from 0 to 63, as said below
- page_slot: int32 [512], P('req'), may hold values from 0 to 7, as said below
Outputs:
- out: bfloat16 [512, 64, 1152], P('rep', 'req')
- new_pages: bfloat16 [512, 2, 8, 384], P(('req', 'rep'))
Inputs may be any that keep to these rules, and one draw needn't show every extreme that they name: `cache`: no structure is promised. page_table[r, j, s] is the index, among the 16 pages of device j of request r's owner, of the request's logical page s * 4 + j; requests of one owner in aligned blocks of 4 share the pages of logical pages below 16; all other pages are distinct. `cache_len`: every owner holds a request of the largest length. parents[r, 0] = 0; node t >= 1 has depth (t * 7 + 62) // 63 and its parent is a node of the depth before. accept_leaf names a node of depth 8 - 1. `page_slot`: the 8 requests of each owner take each slot once.
All inputs are finite; a program needn't handle non-finite values.
Results may differ from a plain program's by a relative error of at most 0.019.
The roundings to bfloat16 on the way count: a program that leaves them out, or rounds other values in their place, can miss the bound.
Values may be sent and summed in bfloat16 or wider, within the bound.
A program may use at most 128 MiB of HBM per device.

v0:
```python
import jax
import jax.numpy as jnp
from jax import lax
from jax.sharding import PartitionSpec as P

QUERY_HEADS = 18
KEY_VALUE_HEADS = 6
ACC = 8
SCALE = 0.125
EPSILON = 1e-05
THETA = 10000.0


def apply_rotation(values, token_positions, head_count):
    head_columns = values.shape[-1] // head_count
    half_width = head_columns // 2
    shaped = values.reshape(values.shape[:-1] + (head_count, head_columns))
    frequency = THETA ** (-jnp.arange(half_width, dtype=jnp.float32) / half_width)
    angles = token_positions.astype(jnp.float32)[..., None] * frequency
    cosine = jnp.cos(angles)[..., None, :]
    sines = jnp.sin(angles)[..., None, :]
    front_half = shaped[..., :half_width]
    back_half = shaped[..., half_width:]
    turned = jnp.concatenate(
        [front_half * cosine - back_half * sines, back_half * cosine + front_half * sines], axis=-1
    )
    return turned.reshape(values.shape)


def ancestors(parents):
    tree_length = parents.shape[-1]
    identity = jnp.eye(tree_length, dtype=jnp.float32)
    linked = jax.nn.one_hot(parents, tree_length, dtype=jnp.float32)
    reached = jnp.minimum(identity + linked, 1.0)
    for doubling in range(tree_length.bit_length()):
        reached = jnp.minimum(
            jnp.einsum("rts,rsu->rtu", reached, reached, precision=lax.Precision.HIGHEST), 1.0
        )
    return reached


def rms_scaled(values_in, gain):
    scaling = lax.rsqrt(jnp.mean(values_in * values_in, axis=-1, keepdims=True) + EPSILON)
    return (values_in * scaling * gain).astype(jnp.bfloat16)


def project(hidden, norm_gain, w_qkv):
    normed = rms_scaled(hidden.astype(jnp.float32), norm_gain)
    product = jnp.dot(
        normed.reshape(-1, hidden.shape[-1]), w_qkv, preferred_element_type=jnp.float32
    )
    return product.astype(jnp.bfloat16).reshape(hidden.shape[:-1] + (w_qkv.shape[1],))


def attend_part(query_matrix, key_matrix, value_matrix, allowed):
    tree_length = query_matrix.shape[0]
    head_columns = key_matrix.shape[-1]
    grouped_queries = query_matrix.reshape(
        tree_length, KEY_VALUE_HEADS, QUERY_HEADS // KEY_VALUE_HEADS, head_columns
    )
    scores = (
        jnp.einsum(
            "tgrd,sgd->gtrs", grouped_queries, key_matrix, preferred_element_type=jnp.float32
        )
        * SCALE
    )
    scores = jnp.where(allowed[None, :, None, :], scores, -jnp.inf)
    peaks = jnp.max(scores, axis=-1)
    weights = jnp.exp(scores - peaks[..., None])
    totals = jnp.sum(weights, axis=-1)
    summed = jnp.einsum(
        "gtrs,sgd->tgrd",
        weights.astype(jnp.bfloat16),
        value_matrix,
        preferred_element_type=jnp.float32,
    )
    peaks = jnp.transpose(peaks, (1, 0, 2)).reshape(tree_length, QUERY_HEADS)
    totals = jnp.transpose(totals, (1, 0, 2)).reshape(tree_length, QUERY_HEADS)
    return (peaks, totals, summed.reshape(tree_length, QUERY_HEADS * head_columns))


def join_parts(front_part, back_part):
    highest = jnp.maximum(front_part[0], back_part[0])
    front_scale = jnp.exp(front_part[0] - highest)
    back_scale = jnp.exp(back_part[0] - highest)
    totals = front_part[1] * front_scale + back_part[1] * back_scale
    shape_sum = front_part[2].shape
    split_shape = shape_sum[:-1] + (QUERY_HEADS, -1)
    summed = (
        front_part[2].reshape(split_shape) * front_scale[..., None]
        + back_part[2].reshape(split_shape) * back_scale[..., None]
    )
    return (highest, totals, summed.reshape(shape_sum))


def owner_partials(
    queries_all, local_key_rows, local_value_rows, own_reach, cache, page_list, cache_len, own_start
):
    rep_index = lax.axis_index("rep")
    rep_count = lax.axis_size("rep")
    requests = queries_all.shape[0]
    tree_length = queries_all.shape[1]
    owner_page_count = local_key_rows.shape[0]
    slots_count = page_list.shape[1]
    page_length = cache.shape[2]
    head_columns = local_key_rows.shape[-1] // KEY_VALUE_HEADS
    logical = (
        jnp.arange(slots_count, dtype=jnp.int32)[:, None] * rep_count + rep_index
    ) * page_length + jnp.arange(page_length, dtype=jnp.int32)[None, :]
    logical = logical.reshape(slots_count * page_length)

    def per_request(request_item):
        query_matrix, page_ids, cache_end = request_item
        collected_pages = cache[page_ids]
        key_matrix = collected_pages[:, 0].reshape(
            slots_count * page_length, KEY_VALUE_HEADS, head_columns
        )
        value_matrix = collected_pages[:, 1].reshape(
            slots_count * page_length, KEY_VALUE_HEADS, head_columns
        )
        visible = jnp.broadcast_to(
            (logical < cache_end)[None, :], (tree_length, slots_count * page_length)
        )
        return attend_part(query_matrix, key_matrix, value_matrix, visible)

    cached = lax.map(per_request, (queries_all, page_list, cache_len))
    own_queries = lax.dynamic_slice_in_dim(queries_all, own_start, owner_page_count, 0)
    drafted = jax.vmap(attend_part)(
        own_queries,
        local_key_rows.reshape(owner_page_count, tree_length, KEY_VALUE_HEADS, head_columns),
        local_value_rows.reshape(owner_page_count, tree_length, KEY_VALUE_HEADS, head_columns),
        own_reach > 0.5,
    )
    blanks = (
        jnp.full((requests, tree_length, QUERY_HEADS), -jnp.inf, jnp.float32),
        jnp.zeros((requests, tree_length, QUERY_HEADS), jnp.float32),
        jnp.zeros((requests, tree_length, queries_all.shape[2]), jnp.float32),
    )
    placed = tuple(
        (
            lax.dynamic_update_slice_in_dim(blank_part, drafted_part, own_start, 0)
            for blank_part, drafted_part in zip(blanks, drafted)
        )
    )
    return join_parts(cached, placed)


def path_rows(key_matrix, value_matrix, reached, depths, leaf_ids):
    tree_length = reached.shape[-1]
    leaf_hot = jax.nn.one_hot(leaf_ids, tree_length, dtype=jnp.float32)
    on_path = jnp.einsum("rt,rts->rs", leaf_hot, reached, precision=lax.Precision.HIGHEST)
    level_hot = (depths[:, None, :] == jnp.arange(ACC, dtype=jnp.int32)[None, :, None]).astype(
        jnp.float32
    )
    selector = (on_path[:, None, :] * level_hot).astype(jnp.bfloat16)
    stacked = jnp.stack([key_matrix, value_matrix], axis=1)
    return jnp.einsum(
        "ras,rbsc->rbac", selector, stacked, preferred_element_type=jnp.float32
    ).astype(jnp.bfloat16)


def place_rows(rows, page_slot, own_start, owner_page_count):
    slot_ids = own_start + jnp.arange(owner_page_count, dtype=jnp.int32)
    chooser = (page_slot[None, :] == slot_ids[:, None]).astype(jnp.bfloat16)
    return jnp.einsum("pr,rbac->pbac", chooser, rows, preferred_element_type=jnp.float32).astype(
        jnp.bfloat16
    )


def scale_sums(peaks, peak_all, totals, summed):
    factors = jnp.exp(peaks - peak_all)
    split_shape = summed.shape[:-1] + (QUERY_HEADS, -1)
    scaled = (summed.reshape(split_shape) * factors[..., None]).reshape(summed.shape)
    return (scaled, totals * factors)


def body(
    hidden,
    norm_gain,
    w_qkv,
    w_out,
    ffn_gain,
    w_gate,
    w_up,
    w_down,
    cache,
    page_table,
    cache_len,
    parents,
    accept_leaf,
    page_slot,
):
    block_rows, draft_part, model_width = hidden.shape
    channels = w_qkv.shape[1]
    query_columns = w_out.shape[0]
    key_value_columns = (channels - query_columns) // 2
    req_count = lax.axis_size("req")
    rep_count = lax.axis_size("rep")
    rep_index = lax.axis_index("rep")
    requests = cache_len.shape[0]
    owner_page_count = requests // rep_count
    tree_length = parents.shape[1]
    own_start = rep_index * owner_page_count
    projected_rows = project(hidden, norm_gain, w_qkv)
    reached = ancestors(parents)
    depths = jnp.sum(reached, axis=-1).astype(jnp.int32) - 1
    token_positions = cache_len[:, None] + depths
    page_list = page_table[:, 0, :]
    own_reach = lax.dynamic_slice_in_dim(reached, own_start, owner_page_count, 0)
    fanned = lax.all_gather(projected_rows, "rep", axis=0, tiled=True)
    arranged = fanned.reshape(requests, req_count, draft_part, channels)
    owned_pages = lax.all_to_all(arranged, "req", split_axis=1, concat_axis=2, tiled=True).reshape(
        requests, tree_length, channels
    )
    queries_all = apply_rotation(
        owned_pages[..., :query_columns].astype(jnp.float32), token_positions, QUERY_HEADS
    ).astype(jnp.bfloat16)
    keys_all = apply_rotation(
        owned_pages[..., query_columns : query_columns + key_value_columns].astype(jnp.float32),
        token_positions,
        KEY_VALUE_HEADS,
    ).astype(jnp.bfloat16)
    values_all = owned_pages[..., query_columns + key_value_columns :]
    local_key_rows = lax.dynamic_slice_in_dim(keys_all, own_start, owner_page_count, 0)
    local_value_rows = lax.dynamic_slice_in_dim(values_all, own_start, owner_page_count, 0)
    peaks, totals, summed = owner_partials(
        queries_all,
        local_key_rows,
        local_value_rows,
        own_reach,
        cache,
        page_list,
        cache_len,
        own_start,
    )
    returned = (
        lax.all_to_all(
            peaks.reshape(requests, 1, tree_length, QUERY_HEADS),
            "req",
            split_axis=2,
            concat_axis=1,
            tiled=True,
        ),
        lax.all_to_all(
            totals.reshape(requests, 1, tree_length, QUERY_HEADS),
            "req",
            split_axis=2,
            concat_axis=1,
            tiled=True,
        ),
        lax.all_to_all(
            summed.reshape(requests, 1, tree_length, query_columns),
            "req",
            split_axis=2,
            concat_axis=1,
            tiled=True,
        ),
    )
    back_peaks = returned[0].reshape(requests * req_count, draft_part, QUERY_HEADS)
    back_totals = returned[1].reshape(requests * req_count, draft_part, QUERY_HEADS)
    back_sums = returned[2].reshape(requests * req_count, draft_part, query_columns)
    peak_all = lax.pmax(back_peaks, "rep")
    scaled, scaled_totals = scale_sums(back_peaks, peak_all, back_totals, back_sums)
    shared = (
        lax.psum_scatter(scaled, "rep", scatter_dimension=0, tiled=True),
        lax.psum_scatter(scaled_totals, "rep", scatter_dimension=0, tiled=True),
    )
    attended = (
        (shared[0].reshape(block_rows, draft_part, QUERY_HEADS, -1) / shared[1][..., None])
        .reshape(block_rows, draft_part, query_columns)
        .astype(jnp.bfloat16)
    )
    all_rows = path_rows(keys_all, values_all, reached, depths, accept_leaf)
    mixed = jnp.dot(attended.reshape(-1, query_columns), w_out, preferred_element_type=jnp.float32)
    residual = (mixed + hidden.reshape(-1, model_width).astype(jnp.float32)).astype(jnp.bfloat16)
    residual_wide = residual.astype(jnp.float32)
    ffn_in = rms_scaled(residual_wide, ffn_gain).reshape(hidden.shape)
    collected_pages = lax.all_gather(ffn_in, "rep", axis=0, tiled=True)
    rows_in = collected_pages.reshape(-1, model_width)
    gate = jnp.dot(rows_in, w_gate, preferred_element_type=jnp.float32)
    up = jnp.dot(rows_in, w_up, preferred_element_type=jnp.float32)
    activated = (jax.nn.silu(gate) * up).astype(jnp.bfloat16)
    ffn_sum = lax.psum_scatter(
        jnp.dot(activated, w_down, preferred_element_type=jnp.float32).reshape(
            block_rows * lax.axis_size("rep"), draft_part, model_width
        ),
        "rep",
        scatter_dimension=0,
        tiled=True,
    )
    out = (ffn_sum + residual_wide.reshape(hidden.shape)).astype(jnp.bfloat16)
    new_pages = place_rows(all_rows, page_slot, own_start, owner_page_count)
    return (out, new_pages)


def solution(mesh):
    placed = (
        P("rep", "req", None),
        P(),
        P(),
        P(),
        P(),
        P(None, "rep"),
        P(None, "rep"),
        P("rep", None),
        P(("req", "rep"), None, None, None),
        P("req", "rep", None),
        P("req"),
        P("req", None),
        P("req"),
        P("req"),
    )
    return jax.shard_map(
        body,
        mesh=mesh,
        in_specs=placed,
        out_specs=(P("rep", "req", None), P(("req", "rep"), None, None, None)),
        check_vma=False,
    )
```

profile of v0, /device:TPU:1, one launch (start us, length us, event | category | flops | bytes accessed | tf_op | source)
XLA Modules:
  0.0 617.9 jit_solution(11852952766045524678)
XLA Ops:
  8.5 4.1 convolution_convert_fusion
  12.6 36.0 %all-gather.5.cloned.1.call-done = bf16[512,1920]{1,0:T(8,128)(2,1)} async-done(((bf16[128,1920]{1,0:T(8,128)(2,1)}), bf16[512,1920]{1,0:T(8,128)(2,1)}) %all-gather.5.cloned.1.call-update) | async-done | bytes 1966096 | tf_op jit(solution)/shard_map/all_gather | solution.py:210
  48.6 4.0 copy.113
  52.5 11.8 %all-to-all-start = ((bf16[8,64,1,1920]{3,0,2,1:T(8,128)(2,1)}), bf16[8,64,1,1920]{3,0,2,1:T(8,128)(2,1)}, u32[]{:S(2)}, u32[]{:S(2)}) async-start(bf16[8,64,1,1920]{3,0,2,1:T(8,128)(2,1)} %copy.113), calls=%async_computation | async-start | bytes 3932160 | tf_op jit(solution)/shard_map/all_to_all | solution.py:212
  71.9 40.4 %all-to-all-done = bf16[8,64,1,1920]{3,0,2,1:T(8,128)(2,1)} async-done(((bf16[8,64,1,1920]{3,0,2,1:T(8,128)(2,1)}), bf16[8,64,1,1920]{3,0,2,1:T(8,128)(2,1)}, u32[]{:S(2)}, u32[]{:S(2)}) %all-to-all-start) | async-done | bytes 1966112 | tf_op jit(solution)/shard_map/all_to_all | solution.py:212
  118.7 3.1 multiply_subtract_fusion
  125.6 5.5 reshape.319
  131.1 6.6 %subtract_convert_fusion = (bf16[8,64,18,32]{3,2,1,0:T(8,128)(2,1)S(1)}, bf16[8,64,18,32]{3,2,1,0:T(8,128)(2,1)S(1)}) fusion(f32[8,64,18,64]{3,2,1,0:T(8,128)} %reshape.319, f32[8,64,32]{2,1,0:T(8,128)S(1)} %copy-done.3, f32[8,64,32]{2,1,0:T(8,128)S(1)} %copy-done.2), kind=kLoop, calls=%fused_computation.28 | loop fusion | flops 2359296 | bytes 3670016 | tf_op jit(solution)/shard_map/convert.3
  137.7 3.5 pad_maximum_fusion
  141.2 4.7 convert_element_type.116
  157.6 225.7 %while.15 = (s32[]{:T(128)}, f32[8,64,18]{1,0,2:T(8,128)}, f32[8,64,18]{1,0,2:T(8,128)}, f32[8,64,1152]{2,1,0:T(8,128)}, s32[8]{0:T(128)}, /*index=5*/bf16[8,64,...) while((s32[]{:T(128)}, f32[8,64,18]{1,0,2:T(8,128)}, ...), condition=%wide.region_5.6_spmd.clone, body=%wide.region_2.5_spmd.clone.sunk | while | flops 196853776 | bytes 19970600 | solution.py:126
  160.2 3.6 gather_fusion
  170.2 3.2 fusion.110
  176.2 2.9 fusion.112
  188.4 3.6 gather_fusion
  198.4 3.2 fusion.110
  216.7 3.6 gather_fusion
  226.6 3.2 fusion.110
  232.6 2.9 fusion.112
  244.9 3.6 gather_fusion
  254.8 3.2 fusion.110
  273.1 3.6 gather_fusion
  283.0 3.1 fusion.110
  301.3 3.6 gather_fusion
  311.2 3.1 fusion.110
  317.2 2.9 fusion.112
  329.5 3.6 gather_fusion
  339.4 3.2 fusion.110
  357.7 3.6 gather_fusion
  367.6 3.1 fusion.110
  387.7 6.1 all-to-all-start.2
  396.3 3.8 mul.244
  400.1 5.3 mul.245
  405.5 3.8 mul.248
  409.3 5.3 mul.249
  415.7 10.6 %all-to-all-start.3 = ((f32[64,1,144]{2,1,0:T(1,128)}), f32[64,1,144]{2,1,0:T(1,128)S(1)}, u32[]{:S(2)}, u32[]{:S(2)}) async-start(f32[64,1,144]{2,1,0:T(1,128)} %reshape.357), calls=%async_computation.4 | async-start | bytes 131072 | tf_op jit(solution)/shard_map/all_to_all | solution.py:244
  426.3 4.2 bitcast_add_fusion
  436.0 7.9 %all-to-all-start.1 = ((f32[8,1,64,1152]{3,0,1,2:T(8,128)}), f32[8,1,64,1152]{3,0,1,2:T(8,128)}, u32[]{:S(2)}, u32[]{:S(2)}) async-start(f32[8,1,64,1152]{3,0,1,2:T(8,128)} %copy.132), calls=%async_computation.1 | async-start | bytes 4718592 | tf_op jit(solution)/shard_map/all_to_all | solution.py:251
  446.9 13.3 %pmax.7 = f32[512,1,18]{0,1,2:T(1,128)S(1)} all-reduce(f32[512,1,18]{0,1,2:T(1,128)S(1)} %reshape.309), channel_id=1, replica_groups=mesh['req'=64,'rep'=4] {'rep'}, use_global_device_ids=true, to_apply=%region_7.8 | all-reduce | flops 9216 | bytes 73728 | tf_op jit(solution)/shard_map/pmax | solution.py:262
  462.0 3.1 copy.136
  465.1 4.1 copy.158
  469.3 5.2 bitcast_reduce_fusion
  474.5 25.9 %all-to-all-done.1 = f32[8,1,64,1152]{3,0,1,2:T(8,128)} async-done(((f32[8,1,64,1152]{3,0,1,2:T(8,128)}), f32[8,1,64,1152]{3,0,1,2:T(8,128)}, u32[]{:S(2)}, u32[]{:S(2)}) %all-to-all-start.1) | async-done | bytes 2359328 | tf_op jit(solution)/shard_map/all_to_all | solution.py:251
  510.0 26.1 %reduce-scatter.6.cloned.1.call-done = f32[128,1,1152]{2,0,1:T(8,128)} async-done(((f32[512,1,1152]{2,0,1:T(8,128)}), f32[128,1,1152]{2,0,1:T(8,128)}) %reduce-scatter.6.cloned.1.call-update) | async-done | bytes 589840 | tf_op jit(solution)/shard_map/reduce_scatter | solution.py:265
  539.1 24.7 %all-gather.7.cloned.1.call-done = bf16[512,1152]{1,0:T(8,128)(2,1)} async-done(((bf16[128,1152]{1,0:T(8,128)(2,1)}), bf16[512,1152]{1,0:T(8,128)(2,1)}) %all-gather.7.cloned.1.call-update) | async-done | bytes 1179664 | tf_op jit(solution)/shard_map/all_gather | solution.py:278
  563.8 3.2 fusion.77
  567.0 5.0 convolution_bitcast_fusion
  577.9 31.4 %reduce-scatter.8.cloned.1.call-done = f32[128,1,1152]{2,0,1:T(8,128)} async-done(((f32[512,1,1152]{2,0,1:T(8,128)}), f32[128,1,1152]{2,0,1:T(8,128)}) %reduce-scatter.8.cloned.1.call-update) | async-done | bytes 589840 | tf_op jit(solution)/shard_map/reduce_scatter | solution.py:283
  (308 shorter events, 231.5 us)
Async XLA Ops:
  7.2 529.0 %copy-start = (bf16[1152,1152]{1,0:T(8,128)(2,1)S(1)}, bf16[1152,1152]{1,0:T(8,128)(2,1)}, u32[]{:S(2)}) copy-start(bf16[1152,1152]{1,0:T(8,128)(2,1)} %param.19) | copy-start | bytes 7962628
  7.2 41.4 %all-gather.5.cloned.1.call-start = ((), (), s32[]{:S(2)}) async-start(), calls=%async_computation.9 | async-start | bytes 2457600 | tf_op jit(solution)/shard_map/all_gather | solution.py:210
  52.5 11.8 %copy-start.16 = (s32[8,64]{1,0:T(8,128)S(1)}, s32[8,64]{1,0:T(8,128)}, u32[]{:S(2)}) copy-start(s32[8,64]{1,0:T(8,128)} %param.27) | copy-start | bytes 6148
  52.5 59.8 %all-to-all-start = ((bf16[8,64,1,1920]{3,0,2,1:T(8,128)(2,1)}), bf16[8,64,1,1920]{3,0,2,1:T(8,128)(2,1)}, u32[]{:S(2)}, u32[]{:S(2)}) async-start(bf16[8,64,1,1920]{3,0,2,1:T(8,128)(2,1)} %copy.113), calls=%async_computation | async-start | bytes 3932160 | tf_op jit(solution)/shard_map/all_to_all | solution.py:212
  64.9 3.3 copy-start.15
  67.4 0.7 copy-start.5
  125.6 5.5 copy-start.2
  125.6 5.5 copy-start.3
  157.6 10.0 %copy-start.13 = (s32[8,5]{1,0:T(8,128)}, s32[8,5]{1,0:T(8,128)S(1)}, u32[]{:S(2)}) copy-start(s32[8,5]{1,0:T(8,128)S(1)} %get-tuple-element.250) | copy-start | bytes 484 | tf_op jit(solution)/shard_map/while
  179.3 6.5 %copy-start.14 = (s32[8,5]{1,0:T(8,128)S(1)}, s32[8,5]{1,0:T(8,128)}, u32[]{:S(2)}) copy-start(s32[8,5]{1,0:T(8,128)} %copy-done.13) | copy-start | bytes 484 | tf_op jit(solution)/shard_map/while
  185.8 10.0 %copy-start.13 = (s32[8,5]{1,0:T(8,128)}, s32[8,5]{1,0:T(8,128)S(1)}, u32[]{:S(2)}) copy-start(s32[8,5]{1,0:T(8,128)S(1)} %get-tuple-element.250) | copy-start | bytes 484 | tf_op jit(solution)/shard_map/while
  207.5 6.5 %copy-start.14 = (s32[8,5]{1,0:T(8,128)S(1)}, s32[8,5]{1,0:T(8,128)}, u32[]{:S(2)}) copy-start(s32[8,5]{1,0:T(8,128)} %copy-done.13) | copy-start | bytes 484 | tf_op jit(solution)/shard_map/while
  214.0 10.0 %copy-start.13 = (s32[8,5]{1,0:T(8,128)}, s32[8,5]{1,0:T(8,128)S(1)}, u32[]{:S(2)}) copy-start(s32[8,5]{1,0:T(8,128)S(1)} %get-tuple-element.250) | copy-start | bytes 484 | tf_op jit(solution)/shard_map/while
  235.8 6.5 %copy-start.14 = (s32[8,5]{1,0:T(8,128)S(1)}, s32[8,5]{1,0:T(8,128)}, u32[]{:S(2)}) copy-start(s32[8,5]{1,0:T(8,128)} %copy-done.13) | copy-start | bytes 484 | tf_op jit(solution)/shard_map/while
  242.2 10.0 %copy-start.13 = (s32[8,5]{1,0:T(8,128)}, s32[8,5]{1,0:T(8,128)S(1)}, u32[]{:S(2)}) copy-start(s32[8,5]{1,0:T(8,128)S(1)} %get-tuple-element.250) | copy-start | bytes 484 | tf_op jit(solution)/shard_map/while
  264.0 6.4 %copy-start.14 = (s32[8,5]{1,0:T(8,128)S(1)}, s32[8,5]{1,0:T(8,128)}, u32[]{:S(2)}) copy-start(s32[8,5]{1,0:T(8,128)} %copy-done.13) | copy-start | bytes 484 | tf_op jit(solution)/shard_map/while
  270.4 10.0 %copy-start.13 = (s32[8,5]{1,0:T(8,128)}, s32[8,5]{1,0:T(8,128)S(1)}, u32[]{:S(2)}) copy-start(s32[8,5]{1,0:T(8,128)S(1)} %get-tuple-element.250) | copy-start | bytes 484 | tf_op jit(solution)/shard_map/while
  292.2 6.4 %copy-start.14 = (s32[8,5]{1,0:T(8,128)S(1)}, s32[8,5]{1,0:T(8,128)}, u32[]{:S(2)}) copy-start(s32[8,5]{1,0:T(8,128)} %copy-done.13) | copy-start | bytes 484 | tf_op jit(solution)/shard_map/while
  298.6 10.0 %copy-start.13 = (s32[8,5]{1,0:T(8,128)}, s32[8,5]{1,0:T(8,128)S(1)}, u32[]{:S(2)}) copy-start(s32[8,5]{1,0:T(8,128)S(1)} %get-tuple-element.250) | copy-start | bytes 484 | tf_op jit(solution)/shard_map/while
  320.4 6.4 %copy-start.14 = (s32[8,5]{1,0:T(8,128)S(1)}, s32[8,5]{1,0:T(8,128)}, u32[]{:S(2)}) copy-start(s32[8,5]{1,0:T(8,128)} %copy-done.13) | copy-start | bytes 484 | tf_op jit(solution)/shard_map/while
  326.8 10.0 %copy-start.13 = (s32[8,5]{1,0:T(8,128)}, s32[8,5]{1,0:T(8,128)S(1)}, u32[]{:S(2)}) copy-start(s32[8,5]{1,0:T(8,128)S(1)} %get-tuple-element.250) | copy-start | bytes 484 | tf_op jit(solution)/shard_map/while
  348.6 6.5 %copy-start.14 = (s32[8,5]{1,0:T(8,128)S(1)}, s32[8,5]{1,0:T(8,128)}, u32[]{:S(2)}) copy-start(s32[8,5]{1,0:T(8,128)} %copy-done.13) | copy-start | bytes 484 | tf_op jit(solution)/shard_map/while
  355.0 10.0 %copy-start.13 = (s32[8,5]{1,0:T(8,128)}, s32[8,5]{1,0:T(8,128)S(1)}, u32[]{:S(2)}) copy-start(s32[8,5]{1,0:T(8,128)S(1)} %get-tuple-element.250) | copy-start | bytes 484 | tf_op jit(solution)/shard_map/while
  376.8 6.5 %copy-start.14 = (s32[8,5]{1,0:T(8,128)S(1)}, s32[8,5]{1,0:T(8,128)}, u32[]{:S(2)}) copy-start(s32[8,5]{1,0:T(8,128)} %copy-done.13) | copy-start | bytes 484 | tf_op jit(solution)/shard_map/while
  383.3 12.1 %copy-start.4 = (f32[2,1,64,1152]{3,2,0,1:T(8,128)S(1)}, f32[2,1,64,1152]{3,2,0,1:T(8,128)}, u32[]{:S(2)}) copy-start(f32[2,1,64,1152]{3,2,0,1:T(8,128)} %copy.130) | copy-start | bytes 1769476
  387.7 8.5 %copy-start.10 = (f32[8,64,18]{1,0,2:T(8,128)S(1)}, f32[8,64,18]{1,0,2:T(8,128)}, u32[]{:S(2)}) copy-start(f32[8,64,18]{1,0,2:T(8,128)} %get-tuple-element.133) | copy-start | bytes 110596
  387.7 28.0 %all-to-all-start.2 = ((f32[64,1,144]{2,1,0:T(1,128)}), f32[64,1,144]{2,1,0:T(1,128)S(1)}, u32[]{:S(2)}, u32[]{:S(2)}) async-start(f32[64,1,144]{2,1,0:T(1,128)} %reshape.355), calls=%async_computation.2 | async-start | bytes 131072 | tf_op jit(solution)/shard_map/all_to_all | solution.py:237
  400.1 5.3 copy-start.9
  409.3 5.3 copy-start.8
  415.7 20.3 %all-to-all-start.3 = ((f32[64,1,144]{2,1,0:T(1,128)}), f32[64,1,144]{2,1,0:T(1,128)S(1)}, u32[]{:S(2)}, u32[]{:S(2)}) async-start(f32[64,1,144]{2,1,0:T(1,128)} %reshape.357), calls=%async_computation.4 | async-start | bytes 131072 | tf_op jit(solution)/shard_map/all_to_all | solution.py:244
  436.0 64.5 %all-to-all-start.1 = ((f32[8,1,64,1152]{3,0,1,2:T(8,128)}), f32[8,1,64,1152]{3,0,1,2:T(8,128)}, u32[]{:S(2)}, u32[]{:S(2)}) async-start(f32[8,1,64,1152]{3,0,1,2:T(8,128)} %copy.132), calls=%async_computation.1 | async-start | bytes 4718592 | tf_op jit(solution)/shard_map/all_to_all | solution.py:251
  443.9 60.7 %reduce-scatter.10.cloned.1.call-start = ((), (), s32[]{:S(2)}) async-start(), calls=%async_computation.11 | async-start | bytes 327680
  474.5 61.7 %reduce-scatter.6.cloned.1.call-start = ((), (), s32[]{:S(2)}) async-start(), calls=%async_computation.7 | async-start | bytes 2949120 | tf_op jit(solution)/shard_map/reduce_scatter | solution.py:265
  500.4 2.4 copy-start.1
  504.5 31.7 %copy-start.7 = (bf16[128,1,1152]{2,0,1:T(8,128)(2,1)S(1)}, bf16[128,1,1152]{2,0,1:T(8,128)(2,1)}, u32[]{:S(2)}) copy-start(bf16[128,1,1152]{2,0,1:T(8,128)(2,1)} %param.16) | copy-start | bytes 884740
  504.5 59.3 %all-gather.7.cloned.1.call-start = ((), (), s32[]{:S(2)}) async-start(), calls=%async_computation.10 | async-start | bytes 1474560 | tf_op jit(solution)/shard_map/all_gather | solution.py:278
  510.0 28.1 %copy-start.11 = (f32[1152]{0:T(1024)S(1)}, f32[1152]{0:T(1024)}, u32[]{:S(2)}) copy-start(f32[1152]{0:T(1024)} %param.20) | copy-start | bytes 13828
  539.0 70.2 %reduce-scatter.8.cloned.1.call-start = ((), (), s32[]{:S(2)}) async-start(), calls=%async_computation.8 | async-start | bytes 2949120 | tf_op jit(solution)/shard_map/reduce_scatter | solution.py:283
  572.0 0.7 copy-start.17
  572.0 1.0 copy-start.6
  572.0 3.7 copy-start.12
  572.0 5.0 copy-start.18
Sparse Core Ops, SparseCore 0:
  12.7 35.8 all-gather.4
  474.6 23.4 reduce-scatter.9
  504.6 31.5 reduce-scatter.5
  539.1 24.6 all-gather.6
  572.2 37.0 reduce-scatter.7
where the time goes:
time: 625 us; the launch traced here: 618 us
  local copies, waits for them, and re-layouts  229 us (37%)
  waiting for transfers between devices  187 us (30%)
  matrix products  70.4 us (11%)
  other arithmetic  66.2 us (11%)
  starting transfers between devices  36.6 us (6%)
  between operations  14.5 us (2%)
  blocking collectives  13.3 us (2%)
    all_to_all x1, waiting for transfers between devices, body(): lax.all_to_all(arranged, 'req', split_axis=1, concat_axis=2, tiled=True)  40.4 us
    all_gather x1, waiting for transfers between devices, body(): fanned = lax.all_gather(projected_rows, 'rep', axis=0, tiled=True)  36 us
    dynamic_update_slice x32, local copies, waits for them, and re-layouts, owner_partials(): cached = lax.map(per_request, (queries_all, page_list, cache_len))  32.5 us
    reduce_scatter x1, waiting for transfers between devices, body(): lax.psum_scatter(jnp.dot(activated, w_down, preferred_element_type=jnp.fl...  31.4 us
    slice x16, local copies, waits for them, and re-layouts, per_request(): collected_pages[:, 1]  30.2 us
    gather x8, local copies, waits for them, and re-layouts, per_request(): collected_pages = cache[page_ids]  28.7 us
    dot_general x9, matrix products, attend_part(): jnp.einsum('tgrd,sgd->gtrs', grouped_queries, key_matrix, preferred_eleme...  26.9 us
    reduce_scatter x1, waiting for transfers between devices, body(): lax.psum_scatter(scaled, 'rep', scatter_dimension=0, tiled=True)  26.1 us
  transfers between devices with their start and end apart: 9, of which 7 were waited for; matrix products, arithmetic and copies ran while one was open for 11% of the time, Pallas kernels for 0%

commit v1 on v0

--- a/solution.py
+++ b/solution.py
@@ -275,7 +275,9 @@
     residual = (mixed + hidden.reshape(-1, model_width).astype(jnp.float32)).astype(jnp.bfloat16)
     residual_wide = residual.astype(jnp.float32)
     ffn_in = rms_scaled(residual_wide, ffn_gain).reshape(hidden.shape)
-    collected_pages = lax.all_gather(ffn_in, "rep", axis=0, tiled=True)
+    collected_pages = jnp.concatenate(
+        lax.all_to_all(jnp.stack([ffn_in] * lax.axis_size("rep")), "rep", 0, 0), axis=0
+    )
     rows_in = collected_pages.reshape(-1, model_width)
     gate = jnp.dot(rows_in, w_gate, preferred_element_type=jnp.float32)
     up = jnp.dot(rows_in, w_up, preferred_element_type=jnp.float32)

time: 625 us -> 616 us (0.986)
  waiting for transfers between devices: 187 us -> 161 us
  blocking collectives: 13.3 us -> 31.6 us
    all_gather x1 -> x0, waiting for transfers between devices: 24.7 us -> none  [body(): collected_pages = lax.all_gather(ffn_in, 'rep', axis=0, tiled=True)]
    all_to_all x0 -> x1, blocking collectives: none -> 18.3 us  [body(): lax.all_to_all(jnp.stack([ffn_in] * lax.axis_size('rep')), 'rep', 0, 0)]
    unnamed x45 -> x49, local copies, waits for them, and re-layouts: 18 us -> 19 us
  transfers between devices with their start and end apart: 9 -> 8, of which waited for: 7 -> 6; matrix products, arithmetic and copies ran while one was open for 11% -> 11% of each run, Pallas kernels for 0% -> 0%
where the time goes in v1:
time: 616 us; the launch traced here: 609 us
  local copies, waits for them, and re-layouts  231 us (38%)
  waiting for transfers between devices  161 us (26%)
  matrix products  68.9 us (11%)
  other arithmetic  65.2 us (11%)
  starting transfers between devices  36.4 us (6%)
  blocking collectives  31.6 us (5%)
  between operations  14.5 us (2%)
    all_to_all x1, waiting for transfers between devices, body(): lax.all_to_all(arranged, 'req', split_axis=1, concat_axis=2, tiled=True)  40.6 us
    all_gather x1, waiting for transfers between devices, body(): fanned = lax.all_gather(projected_rows, 'rep', axis=0, tiled=True)  36 us
    dynamic_update_slice x32, local copies, waits for them, and re-layouts, owner_partials(): cached = lax.map(per_request, (queries_all, page_list, cache_len))  32.6 us
    slice x16, local copies, waits for them, and re-layouts, per_request(): collected_pages[:, 1]  30.2 us
    reduce_scatter x1, waiting for transfers between devices, body(): lax.psum_scatter(jnp.dot(activated, w_down, preferred_element_type=jnp.fl...  29.3 us
    gather x8, local copies, waits for them, and re-layouts, per_request(): collected_pages = cache[page_ids]  28.8 us
    dot_general x9, matrix products, attend_part(): jnp.einsum('tgrd,sgd->gtrs', grouped_queries, key_matrix, preferred_eleme...  27 us
    reduce_scatter x1, waiting for transfers between devices, body(): lax.psum_scatter(scaled, 'rep', scatter_dimension=0, tiled=True)  26.1 us
  transfers between devices with their start and end apart: 8, of which 6 were waited for; matrix products, arithmetic and copies ran while one was open for 11% of the time, Pallas kernels for 0%

profile of v1, /device:TPU:1, one launch (start us, length us, event | category | flops | bytes accessed | tf_op | source)
XLA Modules:
  0.0 608.5 jit_solution(7562464777624329318)
XLA Ops:
  8.5 4.1 convolution_convert_fusion
  12.6 36.0 %all-gather.3.cloned.1.call-done = bf16[512,1920]{1,0:T(8,128)(2,1)} async-done(((bf16[128,1920]{1,0:T(8,128)(2,1)}), bf16[512,1920]{1,0:T(8,128)(2,1)}) %all-gather.3.cloned.1.call-update) | async-done | bytes 1966096 | tf_op jit(solution)/shard_map/all_gather | solution.py:210
  48.6 3.9 copy.113
  52.5 11.6 %all-to-all-start = ((bf16[8,64,1,1920]{3,0,2,1:T(8,128)(2,1)}), bf16[8,64,1,1920]{3,0,2,1:T(8,128)(2,1)}, u32[]{:S(2)}, u32[]{:S(2)}) async-start(bf16[8,64,1,1920]{3,0,2,1:T(8,128)(2,1)} %copy.113), calls=%async_computation | async-start | bytes 3932160 | tf_op jit(solution)/shard_map/all_to_all | solution.py:212
  71.6 40.6 %all-to-all-done = bf16[8,64,1,1920]{3,0,2,1:T(8,128)(2,1)} async-done(((bf16[8,64,1,1920]{3,0,2,1:T(8,128)(2,1)}), bf16[8,64,1,1920]{3,0,2,1:T(8,128)(2,1)}, u32[]{:S(2)}, u32[]{:S(2)}) %all-to-all-start) | async-done | bytes 1966112 | tf_op jit(solution)/shard_map/all_to_all | solution.py:212
  118.5 3.1 multiply_subtract_fusion
  125.4 5.5 reshape.313
  130.9 6.7 %subtract_convert_fusion = (bf16[8,64,18,32]{3,2,1,0:T(8,128)(2,1)S(1)}, bf16[8,64,18,32]{3,2,1,0:T(8,128)(2,1)S(1)}) fusion(f32[8,64,18,64]{3,2,1,0:T(8,128)} %reshape.313, f32[8,64,32]{2,1,0:T(8,128)S(1)} %copy-done.3, f32[8,64,32]{2,1,0:T(8,128)S(1)} %copy-done.2), kind=kLoop, calls=%fused_computation.28 | loop fusion | flops 2359296 | bytes 3670016 | tf_op jit(solution)/shard_map/convert.3
  137.5 3.5 pad_maximum_fusion
  141.0 5.0 convert_element_type.116
  157.8 225.8 %while.15 = (s32[]{:T(128)}, f32[8,64,18]{1,0,2:T(8,128)}, f32[8,64,18]{1,0,2:T(8,128)}, f32[8,64,1152]{2,1,0:T(8,128)}, s32[8]{0:T(128)}, /*index=5*/bf16[8,64,...) while((s32[]{:T(128)}, f32[8,64,18]{1,0,2:T(8,128)}, ...), condition=%wide.region_5.6_spmd.clone, body=%wide.region_2.5_spmd.clone.sunk | while | flops 196853776 | bytes 19970600 | solution.py:126
  160.5 3.6 gather_fusion
  170.4 3.2 fusion.110
  188.7 3.6 gather_fusion
  198.6 3.2 fusion.110
  204.7 2.9 fusion.112
  216.9 3.6 gather_fusion
  226.9 3.1 fusion.110
  245.2 3.6 gather_fusion
  255.1 3.2 fusion.110
  261.1 2.9 fusion.112
  273.4 3.6 gather_fusion
  283.3 3.2 fusion.110
  289.4 2.9 fusion.112
  301.6 3.6 gather_fusion
  311.5 3.2 fusion.110
  317.6 2.9 fusion.112
  329.8 3.6 gather_fusion
  339.7 3.2 fusion.110
  358.1 3.6 gather_fusion
  368.0 3.2 fusion.110
  388.0 6.1 all-to-all-start.2
  396.7 3.8 mul.244
  400.5 5.3 mul.245
  405.9 3.8 mul.248
  409.7 5.3 mul.249
  416.0 10.6 %all-to-all-start.3 = ((f32[64,1,144]{2,1,0:T(1,128)}), f32[64,1,144]{2,1,0:T(1,128)S(1)}, u32[]{:S(2)}, u32[]{:S(2)}) async-start(f32[64,1,144]{2,1,0:T(1,128)} %reshape.349), calls=%async_computation.4 | async-start | bytes 131072 | tf_op jit(solution)/shard_map/all_to_all | solution.py:244
  426.7 4.2 bitcast_add_fusion
  436.3 7.9 %all-to-all-start.1 = ((f32[8,1,64,1152]{3,0,1,2:T(8,128)}), f32[8,1,64,1152]{3,0,1,2:T(8,128)}, u32[]{:S(2)}, u32[]{:S(2)}) async-start(f32[8,1,64,1152]{3,0,1,2:T(8,128)} %copy.132), calls=%async_computation.1 | async-start | bytes 4718592 | tf_op jit(solution)/shard_map/all_to_all | solution.py:251
  447.2 13.3 %pmax.7 = f32[512,1,18]{0,1,2:T(1,128)S(1)} all-reduce(f32[512,1,18]{0,1,2:T(1,128)S(1)} %reshape.305), channel_id=1, replica_groups=mesh['req'=64,'rep'=4] {'rep'}, use_global_device_ids=true, to_apply=%region_7.8 | all-reduce | flops 9216 | bytes 73728 | tf_op jit(solution)/shard_map/pmax | solution.py:262
  462.3 3.1 copy.136
  465.5 4.1 copy.158
  469.6 5.2 bitcast_reduce_fusion
  474.8 25.9 %all-to-all-done.1 = f32[8,1,64,1152]{3,0,1,2:T(8,128)} async-done(((f32[8,1,64,1152]{3,0,1,2:T(8,128)}), f32[8,1,64,1152]{3,0,1,2:T(8,128)}, u32[]{:S(2)}, u32[]{:S(2)}) %all-to-all-start.1) | async-done | bytes 2359328 | tf_op jit(solution)/shard_map/all_to_all | solution.py:251
  510.4 26.1 %reduce-scatter.6.cloned.1.call-done = f32[128,1,1152]{2,0,1:T(8,128)} async-done(((f32[512,1,1152]{2,0,1:T(8,128)}), f32[128,1,1152]{2,0,1:T(8,128)}) %reduce-scatter.6.cloned.1.call-update) | async-done | bytes 589840 | tf_op jit(solution)/shard_map/reduce_scatter | solution.py:265
  538.7 18.3 %all_to_all.20 = bf16[4,128,1,1152]{3,1,2,0:T(8,128)(2,1)S(1)} all-to-all(bf16[4,128,1,1152]{3,1,2,0:T(8,128)(2,1)S(1)} %stack.10), channel_id=1, replica_groups=mesh['req'=64,'rep'=4] {'rep'}, dimensions={0} | all-to-all | bytes 2359296 | tf_op jit(solution)/shard_map/all_to_all | solution.py:279
  559.7 5.0 convolution_bitcast_fusion
  570.6 29.3 %reduce-scatter.8.cloned.1.call-done = f32[128,1,1152]{2,0,1:T(8,128)} async-done(((f32[512,1,1152]{2,0,1:T(8,128)}), f32[128,1,1152]{2,0,1:T(8,128)}) %reduce-scatter.8.cloned.1.call-update) | async-done | bytes 589840 | tf_op jit(solution)/shard_map/reduce_scatter | solution.py:285
  (311 shorter events, 230.6 us)
Async XLA Ops:
  7.2 529.3 %copy-start = (bf16[1152,1152]{1,0:T(8,128)(2,1)S(1)}, bf16[1152,1152]{1,0:T(8,128)(2,1)}, u32[]{:S(2)}) copy-start(bf16[1152,1152]{1,0:T(8,128)(2,1)} %param.19) | copy-start | bytes 7962628
  7.2 41.4 %all-gather.3.cloned.1.call-start = ((), (), s32[]{:S(2)}) async-start(), calls=%async_computation.10 | async-start | bytes 2457600 | tf_op jit(solution)/shard_map/all_gather | solution.py:210
  52.5 11.7 %copy-start.18 = (s32[8,64]{1,0:T(8,128)S(1)}, s32[8,64]{1,0:T(8,128)}, u32[]{:S(2)}) copy-start(s32[8,64]{1,0:T(8,128)} %param.27) | copy-start | bytes 6148
  52.5 59.7 %all-to-all-start = ((bf16[8,64,1,1920]{3,0,2,1:T(8,128)(2,1)}), bf16[8,64,1,1920]{3,0,2,1:T(8,128)(2,1)}, u32[]{:S(2)}, u32[]{:S(2)}) async-start(bf16[8,64,1,1920]{3,0,2,1:T(8,128)(2,1)} %copy.113), calls=%async_computation | async-start | bytes 3932160 | tf_op jit(solution)/shard_map/all_to_all | solution.py:212
  64.7 3.3 copy-start.16
  67.2 0.7 copy-start.5
  125.4 5.5 copy-start.2
  125.4 5.5 copy-start.3
  157.8 10.1 %copy-start.14 = (s32[8,5]{1,0:T(8,128)}, s32[8,5]{1,0:T(8,128)S(1)}, u32[]{:S(2)}) copy-start(s32[8,5]{1,0:T(8,128)S(1)} %get-tuple-element.250) | copy-start | bytes 484 | tf_op jit(solution)/shard_map/while
  179.6 6.5 %copy-start.15 = (s32[8,5]{1,0:T(8,128)S(1)}, s32[8,5]{1,0:T(8,128)}, u32[]{:S(2)}) copy-start(s32[8,5]{1,0:T(8,128)} %copy-done.14) | copy-start | bytes 484 | tf_op jit(solution)/shard_map/while
  186.0 10.1 %copy-start.14 = (s32[8,5]{1,0:T(8,128)}, s32[8,5]{1,0:T(8,128)S(1)}, u32[]{:S(2)}) copy-start(s32[8,5]{1,0:T(8,128)S(1)} %get-tuple-element.250) | copy-start | bytes 484 | tf_op jit(solution)/shard_map/while
  207.8 6.5 %copy-start.15 = (s32[8,5]{1,0:T(8,128)S(1)}, s32[8,5]{1,0:T(8,128)}, u32[]{:S(2)}) copy-start(s32[8,5]{1,0:T(8,128)} %copy-done.14) | copy-start | bytes 484 | tf_op jit(solution)/shard_map/while
  214.3 10.1 %copy-start.14 = (s32[8,5]{1,0:T(8,128)}, s32[8,5]{1,0:T(8,128)S(1)}, u32[]{:S(2)}) copy-start(s32[8,5]{1,0:T(8,128)S(1)} %get-tuple-element.250) | copy-start | bytes 484 | tf_op jit(solution)/shard_map/while
  236.0 6.5 %copy-start.15 = (s32[8,5]{1,0:T(8,128)S(1)}, s32[8,5]{1,0:T(8,128)}, u32[]{:S(2)}) copy-start(s32[8,5]{1,0:T(8,128)} %copy-done.14) | copy-start | bytes 484 | tf_op jit(solution)/shard_map/while
  242.5 10.1 %copy-start.14 = (s32[8,5]{1,0:T(8,128)}, s32[8,5]{1,0:T(8,128)S(1)}, u32[]{:S(2)}) copy-start(s32[8,5]{1,0:T(8,128)S(1)} %get-tuple-element.250) | copy-start | bytes 484 | tf_op jit(solution)/shard_map/while
  264.3 6.5 %copy-start.15 = (s32[8,5]{1,0:T(8,128)S(1)}, s32[8,5]{1,0:T(8,128)}, u32[]{:S(2)}) copy-start(s32[8,5]{1,0:T(8,128)} %copy-done.14) | copy-start | bytes 484 | tf_op jit(solution)/shard_map/while
  270.7 10.1 %copy-start.14 = (s32[8,5]{1,0:T(8,128)}, s32[8,5]{1,0:T(8,128)S(1)}, u32[]{:S(2)}) copy-start(s32[8,5]{1,0:T(8,128)S(1)} %get-tuple-element.250) | copy-start | bytes 484 | tf_op jit(solution)/shard_map/while
  292.5 6.4 %copy-start.15 = (s32[8,5]{1,0:T(8,128)S(1)}, s32[8,5]{1,0:T(8,128)}, u32[]{:S(2)}) copy-start(s32[8,5]{1,0:T(8,128)} %copy-done.14) | copy-start | bytes 484 | tf_op jit(solution)/shard_map/while
  298.9 10.1 %copy-start.14 = (s32[8,5]{1,0:T(8,128)}, s32[8,5]{1,0:T(8,128)S(1)}, u32[]{:S(2)}) copy-start(s32[8,5]{1,0:T(8,128)S(1)} %get-tuple-element.250) | copy-start | bytes 484 | tf_op jit(solution)/shard_map/while
  320.7 6.4 %copy-start.15 = (s32[8,5]{1,0:T(8,128)S(1)}, s32[8,5]{1,0:T(8,128)}, u32[]{:S(2)}) copy-start(s32[8,5]{1,0:T(8,128)} %copy-done.14) | copy-start | bytes 484 | tf_op jit(solution)/shard_map/while
  327.1 10.1 %copy-start.14 = (s32[8,5]{1,0:T(8,128)}, s32[8,5]{1,0:T(8,128)S(1)}, u32[]{:S(2)}) copy-start(s32[8,5]{1,0:T(8,128)S(1)} %get-tuple-element.250) | copy-start | bytes 484 | tf_op jit(solution)/shard_map/while
  348.9 6.5 %copy-start.15 = (s32[8,5]{1,0:T(8,128)S(1)}, s32[8,5]{1,0:T(8,128)}, u32[]{:S(2)}) copy-start(s32[8,5]{1,0:T(8,128)} %copy-done.14) | copy-start | bytes 484 | tf_op jit(solution)/shard_map/while
  355.4 10.1 %copy-start.14 = (s32[8,5]{1,0:T(8,128)}, s32[8,5]{1,0:T(8,128)S(1)}, u32[]{:S(2)}) copy-start(s32[8,5]{1,0:T(8,128)S(1)} %get-tuple-element.250) | copy-start | bytes 484 | tf_op jit(solution)/shard_map/while
  377.2 6.5 %copy-start.15 = (s32[8,5]{1,0:T(8,128)S(1)}, s32[8,5]{1,0:T(8,128)}, u32[]{:S(2)}) copy-start(s32[8,5]{1,0:T(8,128)} %copy-done.14) | copy-start | bytes 484 | tf_op jit(solution)/shard_map/while
  383.6 12.1 %copy-start.4 = (f32[2,1,64,1152]{3,2,0,1:T(8,128)S(1)}, f32[2,1,64,1152]{3,2,0,1:T(8,128)}, u32[]{:S(2)}) copy-start(f32[2,1,64,1152]{3,2,0,1:T(8,128)} %copy.130) | copy-start | bytes 1769476
  388.0 8.5 %copy-start.11 = (f32[8,64,18]{1,0,2:T(8,128)S(1)}, f32[8,64,18]{1,0,2:T(8,128)}, u32[]{:S(2)}) copy-start(f32[8,64,18]{1,0,2:T(8,128)} %get-tuple-element.133) | copy-start | bytes 110596
  388.0 28.0 %all-to-all-start.2 = ((f32[64,1,144]{2,1,0:T(1,128)}), f32[64,1,144]{2,1,0:T(1,128)S(1)}, u32[]{:S(2)}, u32[]{:S(2)}) async-start(f32[64,1,144]{2,1,0:T(1,128)} %reshape.347), calls=%async_computation.2 | async-start | bytes 131072 | tf_op jit(solution)/shard_map/all_to_all | solution.py:237
  400.5 5.3 copy-start.10
  409.7 5.3 copy-start.9
  416.0 20.2 %all-to-all-start.3 = ((f32[64,1,144]{2,1,0:T(1,128)}), f32[64,1,144]{2,1,0:T(1,128)S(1)}, u32[]{:S(2)}, u32[]{:S(2)}) async-start(f32[64,1,144]{2,1,0:T(1,128)} %reshape.349), calls=%async_computation.4 | async-start | bytes 131072 | tf_op jit(solution)/shard_map/all_to_all | solution.py:244
  436.3 64.5 %all-to-all-start.1 = ((f32[8,1,64,1152]{3,0,1,2:T(8,128)}), f32[8,1,64,1152]{3,0,1,2:T(8,128)}, u32[]{:S(2)}, u32[]{:S(2)}) async-start(f32[8,1,64,1152]{3,0,1,2:T(8,128)} %copy.132), calls=%async_computation.1 | async-start | bytes 4718592 | tf_op jit(solution)/shard_map/all_to_all | solution.py:251
  444.2 60.7 %reduce-scatter.10.cloned.1.call-start = ((), (), s32[]{:S(2)}) async-start(), calls=%async_computation.11 | async-start | bytes 327680
  474.8 61.7 %reduce-scatter.6.cloned.1.call-start = ((), (), s32[]{:S(2)}) async-start(), calls=%async_computation.8 | async-start | bytes 2949120 | tf_op jit(solution)/shard_map/reduce_scatter | solution.py:265
  500.8 2.4 copy-start.1
  504.8 31.7 %copy-start.8 = (bf16[128,1,1152]{2,0,1:T(8,128)(2,1)S(1)}, bf16[128,1,1152]{2,0,1:T(8,128)(2,1)}, u32[]{:S(2)}) copy-start(bf16[128,1,1152]{2,0,1:T(8,128)(2,1)} %param.16) | copy-start | bytes 884740
  504.8 95.1 %reduce-scatter.8.cloned.1.call-start = ((), (), s32[]{:S(2)}) async-start(), calls=%async_computation.9 | async-start | bytes 2949120 | tf_op jit(solution)/shard_map/reduce_scatter | solution.py:285
  510.4 28.1 %copy-start.12 = (f32[1152]{0:T(1024)S(1)}, f32[1152]{0:T(1024)}, u32[]{:S(2)}) copy-start(f32[1152]{0:T(1024)} %param.20) | copy-start | bytes 13828
  538.5 19.6 %copy-start.17 = (bf16[1152,384]{1,0:T(8,128)(2,1)S(1)}, bf16[1152,384]{1,0:T(8,128)(2,1)}, u32[]{:S(2)}) copy-start(bf16[1152,384]{1,0:T(8,128)(2,1)} %param.21) | copy-start | bytes 2654212
  557.0 1.0 copy-start.7
  564.7 0.7 copy-start.19
  564.7 1.0 copy-start.6
  564.7 3.7 copy-start.13
  564.7 5.0 copy-start.20
Sparse Core Ops, SparseCore 0:
  12.7 35.8 all-gather.2
  474.9 23.4 reduce-scatter.9
  504.9 31.5 reduce-scatter.5
  564.9 35.0 reduce-scatter.7
